TPU v7x, 256 devices: a whole 4x4x8 slice. The times are simulated.
256 devices in a mesh: seq: 32 (over y, z), head: 8 (over x, core).
Axes of the slice: x: 4, y: 4, z: 8, core: 2. Of those that a mesh axis runs over, the one named last changes fastest.
Arguments:
- hidden: bfloat16 [16384, 8192], P('seq', 'head'), may hold values from -6 to 6
- gain: float32 [8192], replicated, may hold values from 0.25 to 1.75
- key_matrix: bfloat16 [8192, 1024], P(None, 'head'), may hold values from -0.0625 to 0.0625
- value_matrix: bfloat16 [8192, 1024], P(None, 'head'), may hold values from -0.0625 to 0.0625
- queries: bfloat16 [64, 8192], P(None, 'head'), may hold values from -360 to 360
- window_len: int32 [8], P('head'), may hold values from 16 to 64, as said below
- kernel_width: int32 [8], P('head'), may hold values from 1 to 15, as said below
- kept_block_count: int32 [8], P('head'), may hold values from 1 to 64
Outputs:
- block_scores: float32 [8, 128], P('head', 'seq')
- kept_fraction: float32 [8], P('head')
Inputs may be any that keep to these rules, and one draw needn't show every extreme that they name: `window_len`: at least one key-value head uses all 64 window queries. `kernel_width`: odd; at least one key-value head has width 15.
All inputs are finite; a program needn't handle non-finite values.
Results may differ from a plain program's by a relative error of at most 0.0112.
The roundings to bfloat16 on the way count: a program that leaves them out, or rounds other values in their place, can miss the bound.
Values may be sent and summed in bfloat16 or wider, within the bound.
A program may use at most 128 MiB of HBM per device.

v0:
```python
import jax
import jax.numpy as jnp
from jax import lax
from jax.sharding import PartitionSpec as P

BLK = 128
KERNEL_LIMIT = 15


def copy_for_each(x, axis):
    count = lax.axis_size(axis)
    return lax.all_to_all(jnp.broadcast_to(x[None], (count, *x.shape)), axis, 0, 0, tiled=True)


def taken_together(x, axis):
    return copy_for_each(x, axis).sum(axis=0)


def gathered_once(x, axis):
    leaves = jax.tree.leaves(x)
    order = sorted(range(len(leaves)), key=lambda k: -leaves[k].size)
    width = (1, *leaves[order[0]].shape)[-1]
    lines = [
        jnp.pad(leaves[k].reshape(-1), (0, -leaves[k].size % width)).reshape(-1, width)
        for k in order
    ]
    both, at, found = (copy_for_each(jnp.concatenate(lines), axis), 0, {})
    for k, line in zip(order, lines):
        section = both[:, at : at + len(line)].reshape(len(both), -1)
        found[k] = section[:, : leaves[k].size].reshape(-1, *leaves[k].shape)
        at += len(line)
    numbers = iter(range(len(leaves)))
    return jax.tree.map(lambda _: found[next(numbers)], x)


def combined_pairwise(pieces, combine):
    while len(jax.tree.leaves(pieces)[0]) > 1:
        pieces = jax.vmap(combine)(
            *(jax.tree.map(lambda part: part[side::2], pieces) for side in (0, 1))
        )
    return jax.tree.map(lambda part: part[0], pieces)


def joined_all(x, axis, combine):
    pieces = gathered_once(x, axis)
    return combined_pairwise(pieces, combine)


def with_halo(x, sides, width):
    for axis, dim in sides:
        count, length = (lax.axis_size(axis), x.shape[dim])
        up = [(i, (i + 1) % count) for i in range(count - 1)]
        down = [(j, i) for i, j in up]
        last = lax.slice_in_dim(x, length - width, length, axis=dim)
        leading = lax.slice_in_dim(x, 0, width, axis=dim)
        before = lax.ppermute(last, axis, up)
        after = lax.ppermute(leading, axis, down)
        x = jnp.concatenate([before, x, after], axis=dim)
    return x


def laid_out(tiles, dim):
    lengths = list(tiles.shape[1:])
    lengths[dim] *= tiles.shape[0]
    return jnp.moveaxis(tiles, 0, dim).reshape(lengths)


def gathered_copies(x, axis, dim):
    return laid_out(copy_for_each(x, axis), dim)


def rotate(raw, positions):
    half = raw.shape[1] // 2
    freq = 500000.0 ** (-(jnp.arange(half).astype(jnp.float32) * 2.0) / raw.shape[1])
    angle = positions[:, None] * freq[None, :]
    leading_part = raw[:, :half]
    trailing_part = raw[:, half:]
    return jnp.concatenate(
        [
            leading_part * jnp.cos(angle) - trailing_part * jnp.sin(angle),
            trailing_part * jnp.cos(angle) + leading_part * jnp.sin(angle),
        ],
        axis=1,
    )


def combine_stats(earlier, later):
    top = jnp.maximum(earlier[0], later[0])
    total = earlier[1] * jnp.exp(earlier[0] - top) + later[1] * jnp.exp(later[0] - top)
    return (top, total)


def local(
    hidden, gain, key_matrix, value_matrix, queries, window_len, kernel_width, kept_block_count
):
    tok_rows = hidden.shape[0]
    full_width = gain.shape[0]
    head_size = key_matrix.shape[1]
    floats = hidden.astype(jnp.float32)
    sumsq = taken_together(jnp.sum(floats * floats, axis=1), "head")
    inv_rms = lax.rsqrt(sumsq / full_width + 1e-05)
    joined = jnp.concatenate([key_matrix, value_matrix], axis=1)
    normed = (
        lax.all_gather(hidden, "head", axis=1, tiled=True).astype(jnp.float32) * gain[None, :]
    ).astype(jnp.bfloat16)
    projected = jnp.dot(normed, joined, preferred_element_type=jnp.float32)
    projected = projected * inv_rms[:, None]
    tok_index = lax.axis_index("seq") * tok_rows + jnp.arange(tok_rows)
    positions = tok_index.astype(jnp.float32)
    keys = rotate(projected[:, :head_size], positions).astype(jnp.bfloat16)
    vmag = jnp.mean(jnp.abs(projected[:, head_size:]), axis=1)
    window = queries.shape[0]
    group_heads = queries.shape[1] // head_size
    query_rows = queries.reshape(window * group_heads, head_size)
    scores = lax.dot_general(
        query_rows, keys, (((1,), (1,)), ((), ())), preferred_element_type=jnp.float32
    ) * head_size ** (-0.5)
    total_tokens = tok_rows * lax.axis_size("seq")
    limit = jnp.repeat(total_tokens - window + jnp.arange(window), group_heads)
    allowed = tok_index[None, :] <= limit[:, None]
    scores = jnp.where(allowed, scores, jnp.float32(-1e30))
    local_top = jnp.max(scores, axis=1)
    local_expo = jnp.exp(scores - local_top[:, None])
    local_total = jnp.sum(local_expo, axis=1)
    row_top, row_total = joined_all((local_top, local_total), "seq", combine_stats)
    rescale = jnp.exp(local_top - row_top)
    used = (jnp.arange(window) >= window - window_len[0]).astype(jnp.float32)
    row_weight = jnp.repeat(used, group_heads) * rescale / row_total
    column = jnp.dot(row_weight, local_expo, precision=lax.Precision.HIGHEST) * vmag
    reach = (KERNEL_LIMIT - 1) // 2
    padded = with_halo(column, (("seq", 0),), reach)
    kernel_halfspan = (kernel_width[0] - 1) // 2
    pooled = column
    for shift in range(1, reach + 1):
        wider = jnp.maximum(
            jnp.maximum(pooled, padded[reach + shift : reach + shift + tok_rows]),
            padded[reach - shift : reach - shift + tok_rows],
        )
        pooled = jnp.where(shift <= kernel_halfspan, wider, pooled)
    local_blocks = jnp.sum(pooled.reshape(tok_rows // BLK, BLK), axis=1)[None, :]
    everything = gathered_copies(local_blocks, "seq", 1)[0]
    ordered = -jnp.sort(-everything)
    ranks = jnp.arange(ordered.shape[0])
    kept = jnp.sum(jnp.where(ranks < kept_block_count[0], ordered, jnp.float32(0.0)))
    fraction = (kept / jnp.sum(ordered)).reshape(1)
    return (local_blocks, fraction)


def solution(mesh):
    return jax.shard_map(
        local,
        mesh=mesh,
        in_specs=(
            P("seq", "head"),
            P(),
            P(None, "head"),
            P(None, "head"),
            P(None, "head"),
            P("head"),
            P("head"),
            P("head"),
        ),
        out_specs=(P("head", "seq"), P("head")),
        check_vma=False,
    )
```

profile of v0, /device:TPU:2, one launch (start us, length us, event | category | flops | bytes accessed | tf_op | source)
XLA Modules:
  0.0 133.7 jit_solution(4325078742741071064)
XLA Ops:
  7.2 0.7 all-gather.2.cloned.1.call-update
  7.9 1.5 %multiply_reduce_fusion = f32[512]{0:T(512)S(1)} fusion(bf16[512,1024]{1,0:T(8,128)(2,1)} %param.8), kind=kLoop, calls=%fused_computation.6 | loop fusion | flops 1572352 | bytes 1050624 | tf_op jit(solution)/shard_map/reduce_sum | solution.py:100
  9.4 0.6 broadcast_in_dim.21
  10.0 5.5 %all-to-all-start = ((f32[8,1,512]{2,1,0:T(1,128)}), f32[8,1,512]{2,1,0:T(1,128)S(1)}, u32[]{:S(2)}, u32[]{:S(2)}) async-start(f32[8,1,512]{2,1,0:T(1,128)} %broadcast_in_dim.21), calls=%async_computation | async-start | bytes 32768 | tf_op jit(solution)/shard_map/all_to_all | solution.py:12
  15.5 1.0 reshape.69
  16.7 2.8 %all-to-all-done = f32[8,1,512]{2,1,0:T(1,128)S(1)} async-done(((f32[8,1,512]{2,1,0:T(1,128)}), f32[8,1,512]{2,1,0:T(1,128)S(1)}, u32[]{:S(2)}, u32[]{:S(2)}) %all-to-all-start) | async-done | bytes 16416 | tf_op jit(solution)/shard_map/all_to_all | solution.py:12
  19.4 44.7 %all-gather.2.cloned.1.call-done = bf16[512,8192]{1,0:T(8,128)(2,1)} async-done(((bf16[512,1024]{1,0:T(8,128)(2,1)}), bf16[512,8192]{1,0:T(8,128)(2,1)}) %all-gather.2.cloned.1.call-update) | async-done | bytes 8388624 | tf_op jit(solution)/shard_map/all_gather | solution.py:104
  64.2 7.0 %fusion.7 = f32[512,256]{0,1:T(8,128)S(1)} fusion(bf16[8192,128]{1,0:T(8,128)(2,1)} %param.11, bf16[8192,128]{1,0:T(8,128)(2,1)} %param.10, bf16[512,8192]{1,0:T(8,128)(2,1)} %all-gather.2.cloned.1.call-done, f32[8192]{0:T(1024)} %param.9, f32[512]{0:T(512)S(1)} %add_rsqrt_fusion), kind=kOutput, calls=%fused_computation.10 | convolution fusion | flops 2168586240 | bytes 13142016 | tf_op jit(solution)/shard_map/dot_general | solution.py:106
  71.2 0.6 fusion.19
  71.7 0.4 fusion.33
  72.1 0.2 fusion.11
  72.3 0.7 broadcast_in_dim.44
  73.0 9.8 %all-to-all-start.1 = ((f32[32,2,512]{2,1,0:T(2,128)}), f32[32,2,512]{2,1,0:T(2,128)S(1)}, u32[]{:S(2)}, u32[]{:S(2)}) async-start(f32[32,2,512]{2,1,0:T(2,128)} %broadcast_in_dim.44), calls=%async_computation.1 | async-start | bytes 262144 | tf_op jit(solution)/shard_map/all_to_all | solution.py:12
  84.4 9.1 %all-to-all-done.1 = f32[32,2,512]{2,1,0:T(2,128)S(1)} async-done(((f32[32,2,512]{2,1,0:T(2,128)}), f32[32,2,512]{2,1,0:T(2,128)S(1)}, u32[]{:S(2)}, u32[]{:S(2)}) %all-to-all-start.1) | async-done | bytes 131104 | tf_op jit(solution)/shard_map/all_to_all | solution.py:12
  94.1 1.0 fusion.10
  95.2 1.3 collective-permute-start
  96.5 4.5 %collective-permute-start.1 = (f32[7]{0:T(128)S(1)}, f32[7]{0:T(128)S(1)}, u32[]{:S(2)}, u32[]{:S(2)}) collective-permute-start(f32[7]{0:T(128)S(1)} %get-tuple-element.24), channel_id=1, source_target_pairs={{0,8},{8,16},{16,24},{24,32},{32,40},{40,48},{48,56},{56,64},{64,7... | collective-permute-start | bytes 92 | tf_op jit(solution)/shard_map/ppermute | solution.py:56
  101.1 1.3 collective-permute-done.1
  102.4 0.2 bitcast_reduce_fusion
  102.6 0.6 broadcast_in_dim.46
  103.2 7.8 %all-to-all-start.2 = ((f32[32,1,4]{2,1,0:T(1,128)}), f32[32,1,4]{2,1,0:T(1,128)S(1)}, u32[]{:S(2)}, u32[]{:S(2)}) async-start(f32[32,1,4]{2,1,0:T(1,128)} %broadcast_in_dim.46), calls=%async_computation.2 | async-start | bytes 32768 | tf_op jit(solution)/shard_map/all_to_all | solution.py:12
  111.7 9.2 %all-to-all-done.2 = f32[32,1,4]{2,1,0:T(1,128)S(1)} async-done(((f32[32,1,4]{2,1,0:T(1,128)}), f32[32,1,4]{2,1,0:T(1,128)S(1)}, u32[]{:S(2)}, u32[]{:S(2)}) %all-to-all-start.2) | async-done | bytes 544 | tf_op jit(solution)/shard_map/all_to_all | solution.py:12
  121.0 2.6 %sort.15 = (f32[128]{0:T(128)S(1)}, s32[128]{0:T(128)}) sort(f32[128]{0:T(128)S(1)} %neg.20, s32[128]{0:T(128)S(1)} %iota.29), dimensions={0}, to_apply=%region_6.7 | sort | flops 896 | bytes 2048 | tf_op jit(solution)/shard_map/jit(sort)/sort | solution.py:142
  123.6 0.7 fusion.30
  (47 shorter events, 1.3 us)
Async XLA Ops:
  7.2 57.0 %all-gather.2.cloned.1.call-start = ((), (), s32[]{:S(2)}) async-start(), calls=%async_computation.3 | async-start | bytes 9437184 | tf_op jit(solution)/shard_map/all_gather | solution.py:104
  10.0 9.4 %all-to-all-start = ((f32[8,1,512]{2,1,0:T(1,128)}), f32[8,1,512]{2,1,0:T(1,128)S(1)}, u32[]{:S(2)}, u32[]{:S(2)}) async-start(f32[8,1,512]{2,1,0:T(1,128)} %broadcast_in_dim.21), calls=%async_computation | async-start | bytes 32768 | tf_op jit(solution)/shard_map/all_to_all | solution.py:12
  73.0 20.6 %all-to-all-start.1 = ((f32[32,2,512]{2,1,0:T(2,128)}), f32[32,2,512]{2,1,0:T(2,128)S(1)}, u32[]{:S(2)}, u32[]{:S(2)}) async-start(f32[32,2,512]{2,1,0:T(2,128)} %broadcast_in_dim.44), calls=%async_computation.1 | async-start | bytes 262144 | tf_op jit(solution)/shard_map/all_to_all | solution.py:12
  95.2 5.9 %collective-permute-start = (f32[7]{0:T(128)S(1)}, f32[7]{0:T(128)S(1)}, u32[]{:S(2)}, u32[]{:S(2)}) collective-permute-start(f32[7]{0:T(128)S(1)} %get-tuple-element.23), channel_id=1, source_target_pairs={{8,0},{16,8},{24,16},{32,24},{40,32},{48,40},{56,48},{64,56},{72,6... | collective-permute-start | bytes 92 | tf_op jit(solution)/shard_map/ppermute | solution.py:57
  96.5 5.8 %collective-permute-start.1 = (f32[7]{0:T(128)S(1)}, f32[7]{0:T(128)S(1)}, u32[]{:S(2)}, u32[]{:S(2)}) collective-permute-start(f32[7]{0:T(128)S(1)} %get-tuple-element.24), channel_id=1, source_target_pairs={{0,8},{8,16},{16,24},{24,32},{32,40},{40,48},{48,56},{56,64},{64,7... | collective-permute-start | bytes 92 | tf_op jit(solution)/shard_map/ppermute | solution.py:56
  102.6 23.1 %copy-start = (f32[4]{0:T(128)}, f32[4]{0:T(128)S(1)}, u32[]{:S(2)}) copy-start(f32[4]{0:T(128)S(1)} %bitcast_reduce_fusion) | copy-start | bytes 52
  103.2 17.7 %all-to-all-start.2 = ((f32[32,1,4]{2,1,0:T(1,128)}), f32[32,1,4]{2,1,0:T(1,128)S(1)}, u32[]{:S(2)}, u32[]{:S(2)}) async-start(f32[32,1,4]{2,1,0:T(1,128)} %broadcast_in_dim.46), calls=%async_computation.2 | async-start | bytes 32768 | tf_op jit(solution)/shard_map/all_to_all | solution.py:12
Sparse Core Ops, SparseCore 0:
  9.8 54.3 all-gather.1
where the time goes:
time: 134 us
  waiting for transfers between devices  67.7 us (51%)
  starting transfers between devices  29 us (22%)
  between operations  18.7 us (14%)
  matrix products  8.29 us (6%)
  other arithmetic  6.1 us (5%)
  local copies, waits for them, and re-layouts  3.82 us (3%)
    all_gather x1, waiting for transfers between devices, local(): lax.all_gather(hidden, 'head', axis=1, tiled=True).astype(jnp.float32)  44.7 us
    all_to_all x3, starting transfers between devices, copy_for_each(): lax.all_to_all(jnp.broadcast_to(x[None], (count, *x.shape)), axis, 0, 0,...  23.1 us
    all_to_all x3, waiting for transfers between devices, copy_for_each(): lax.all_to_all(jnp.broadcast_to(x[None], (count, *x.shape)), axis, 0, 0,...  21.1 us
    dot_general x1, matrix products, local(): projected = jnp.dot(normed, joined, preferred_element_type=jnp.float32)  6.96 us
    ppermute x1, starting transfers between devices, with_halo(): before = lax.ppermute(last, axis, up)  4.55 us
  transfers between devices with their start and end apart: 6, of which 5 were waited for; matrix products, arithmetic and copies ran while one was open for 3% of the time, Pallas kernels for 0%

commit v1 on v0

--- a/solution.py
+++ b/solution.py
@@ -5,6 +5,27 @@
 
 BLK = 128
 KERNEL_LIMIT = 15
+
+
+def gather_around(x, axis, dim):
+    length, index, width = (lax.axis_size(axis), lax.axis_index(axis), x.shape[dim])
+    upward = [(i, (i + 1) % length) for i in range(length)]
+    left = [(i, (i - 1) % length) for i in range(length)]
+    out = jnp.zeros((*x.shape[:dim], length * width, *x.shape[dim + 1 :]), x.dtype)
+    out = lax.dynamic_update_slice_in_dim(out, x, index * width, axis=dim)
+    from_left = from_right = x
+    half = length // 2
+    for step in range(1, half + 1):
+        from_left = lax.ppermute(from_left, axis, upward)
+        out = lax.dynamic_update_slice_in_dim(
+            out, from_left, (index - step) % length * width, axis=dim
+        )
+        if step < length - half:
+            from_right = lax.ppermute(from_right, axis, left)
+            out = lax.dynamic_update_slice_in_dim(
+                out, from_right, (index + step) % length * width, axis=dim
+            )
+    return out
 
 
 def copy_for_each(x, axis):
@@ -100,9 +121,9 @@
     sumsq = taken_together(jnp.sum(floats * floats, axis=1), "head")
     inv_rms = lax.rsqrt(sumsq / full_width + 1e-05)
     joined = jnp.concatenate([key_matrix, value_matrix], axis=1)
-    normed = (
-        lax.all_gather(hidden, "head", axis=1, tiled=True).astype(jnp.float32) * gain[None, :]
-    ).astype(jnp.bfloat16)
+    normed = (gather_around(hidden, "head", 1).astype(jnp.float32) * gain[None, :]).astype(
+        jnp.bfloat16
+    )
     projected = jnp.dot(normed, joined, preferred_element_type=jnp.float32)
     projected = projected * inv_rms[:, None]
     tok_index = lax.axis_index("seq") * tok_rows + jnp.arange(tok_rows)

time: 134 us -> 127 us (0.948); the launches traced: 134 us -> 124 us
  waiting for transfers between devices: 67.7 us -> 49.9 us
  local copies, waits for them, and re-layouts: 3.82 us -> 19.4 us
  between operations: 18.7 us -> 5.5 us
  starting transfers between devices: 29 us -> 36.4 us
    all_gather x1 -> x0, waiting for transfers between devices: 44.7 us -> none  [local(): lax.all_gather(hidden, 'head', axis=1, tiled=True).astype(jnp.float32)]
    ppermute x0 -> x7, waiting for transfers between devices: none -> 30.5 us  [the longest x4 27.8 us: gather_around(): from_left = lax.ppermute(from_left, axis, upward)]
    dynamic_update_slice x0 -> x8, local copies, waits for them, and re-layouts: none -> 12.3 us  [the longest x4 6.82 us: gather_around(): lax.dynamic_update_slice_in_dim(out, from_left, (index - step) % length *...]
    ppermute x0 -> x7, starting transfers between devices: none -> 4.31 us  [the longest x3 3.98 us: gather_around(): from_right = lax.ppermute(from_right, axis, left)]
    broadcast_in_dim x0 -> x1, local copies, waits for them, and re-layouts: none -> 4.24 us  [gather_around(): jnp.zeros((*x.shape[:dim], length * width, *x.shape[dim + 1:]), x.dtype)]
    all_to_all x3, starting transfers between devices: 23.1 us -> 26.2 us  [copy_for_each(): lax.all_to_all(jnp.broadcast_to(x[None], (count, *x.shape)), axis, 0, 0,...]
    all_to_all x3, waiting for transfers between devices: 21.1 us -> 18.1 us  [copy_for_each(): lax.all_to_all(jnp.broadcast_to(x[None], (count, *x.shape)), axis, 0, 0,...]
  transfers between devices with their start and end apart: 6 -> 12, of which waited for: 5 -> 7; matrix products, arithmetic and copies ran while one was open for 3% -> 15% of each run, Pallas kernels for 0% -> 0%
where the time goes in v1:
time: 127 us; the launch traced here: 124 us
  waiting for transfers between devices  49.9 us (39%)
  starting transfers between devices  36.4 us (29%)
  local copies, waits for them, and re-layouts  19.4 us (15%)
  matrix products  7.14 us (6%)
  other arithmetic  6.1 us (5%)
  between operations  5.5 us (4%)
    ppermute x4, waiting for transfers between devices, gather_around(): from_left = lax.ppermute(from_left, axis, upward)  27.8 us
    all_to_all x3, starting transfers between devices, copy_for_each(): lax.all_to_all(jnp.broadcast_to(x[None], (count, *x.shape)), axis, 0, 0,...  26.2 us
    all_to_all x3, waiting for transfers between devices, copy_for_each(): lax.all_to_all(jnp.broadcast_to(x[None], (count, *x.shape)), axis, 0, 0,...  18.1 us
    dynamic_update_slice x4, local copies, waits for them, and re-layouts, gather_around(): lax.dynamic_update_slice_in_dim(out, from_left, (index - step) % length *...  6.82 us
    dot_general x1, matrix products, local(): projected = jnp.dot(normed, joined, preferred_element_type=jnp.float32)  5.82 us
    ppermute x1, starting transfers between devices, with_halo(): before = lax.ppermute(last, axis, up)  4.55 us
    dynamic_update_slice x3, local copies, waits for them, and re-layouts, gather_around(): lax.dynamic_update_slice_in_dim(out, from_right, (index + step) % length...  4.4 us
    broadcast_in_dim x1, local copies, waits for them, and re-layouts, gather_around(): jnp.zeros((*x.shape[:dim], length * width, *x.shape[dim + 1:]), x.dtype)  4.24 us
  transfers between devices with their start and end apart: 12, of which 7 were waited for; matrix products, arithmetic and copies ran while one was open for 15% of the time, Pallas kernels for 0%

profile of v1, /device:TPU:2, one launch (start us, length us, event | category | flops | bytes accessed | tf_op | source)
XLA Modules:
  0.0 124.4 jit_solution(11803748558204097618)
XLA Ops:
  0.7 1.7 %collective-permute-start.1 = (bf16[512,1024]{1,0:T(8,128)(2,1)}, bf16[512,1024]{1,0:T(8,128)(2,1)S(1)}, u32[]{:S(2)}, u32[]{:S(2)}) collective-permute-start(bf16[512,1024]{1,0:T(8,128)(2,1)} %param.8), channel_id=1, source_target_pairs={{0,7},{1,0},{2,1},{3,2},{4,3},{5,4},{6,5},{7,6},{8,15},{9,8},{10,9... | collective-permute-start | bytes 3145736 | tf_op jit(solution)/shard_map/ppermute | solution.py:24
  2.4 12.7 %collective-permute-done = bf16[512,1024]{1,0:T(8,128)(2,1)S(1)} collective-permute-done((bf16[512,1024]{1,0:T(8,128)(2,1)}, bf16[512,1024]{1,0:T(8,128)(2,1)S(1)}, u32[]{:S(2)}, u32[]{:S(2)}) %collective-permute-start) | collective-permute-done | bytes 1048608 | tf_op jit(solution)/shard_map/ppermute | solution.py:19
  15.1 2.0 %collective-permute-start.3 = (bf16[512,1024]{1,0:T(8,128)(2,1)S(1)}, bf16[512,1024]{1,0:T(8,128)(2,1)}, u32[]{:S(2)}, u32[]{:S(2)}) collective-permute-start(bf16[512,1024]{1,0:T(8,128)(2,1)S(1)} %collective-permute-done.1), channel_id=1, source_target_pairs={{0,7},{1,0},{2,1},{3,2},{4,3},{5,4},{6,5},{7,6},{8,15},{9,8},{10,9... | collective-permute-start | bytes 3145736 | tf_op jit(solution)/shard_map/ppermute | solution.py:24
  17.1 12.3 %collective-permute-done.2 = bf16[512,1024]{1,0:T(8,128)(2,1)} collective-permute-done((bf16[512,1024]{1,0:T(8,128)(2,1)S(1)}, bf16[512,1024]{1,0:T(8,128)(2,1)}, u32[]{:S(2)}, u32[]{:S(2)}) %collective-permute-start.2) | collective-permute-done | bytes 1048608 | tf_op jit(solution)/shard_map/ppermute | solution.py:19
  29.4 1.5 %multiply_reduce_fusion = f32[512]{0:T(512)S(1)} fusion(bf16[512,1024]{1,0:T(8,128)(2,1)} %param.8), kind=kLoop, calls=%fused_computation.6 | loop fusion | flops 1572352 | bytes 1050624 | tf_op jit(solution)/shard_map/reduce_sum | solution.py:121
  31.5 8.9 %all-to-all-start = ((f32[8,1,512]{2,1,0:T(1,128)}), f32[8,1,512]{2,1,0:T(1,128)S(1)}, u32[]{:S(2)}, u32[]{:S(2)}) async-start(f32[8,1,512]{2,1,0:T(1,128)} %broadcast_in_dim.46), calls=%async_computation | async-start | bytes 32768 | tf_op jit(solution)/shard_map/all_to_all | solution.py:33
  40.4 4.2 %broadcast_in_dim.23 = bf16[512,8192]{1,0:T(8,128)(2,1)} broadcast(bf16[]{:T(256)} %constant.112.clone.1), dimensions={} | broadcast | bytes 8388610 | tf_op jit(solution)/shard_map/broadcast_in_dim | solution.py:14
  46.8 1.1 constant_dynamic-update-slice_fusion.6
  48.9 2.3 %constant_dynamic-update-slice_fusion.4 = bf16[512,8192]{1,0:T(8,128)(2,1)} fusion(bf16[512,8192]{1,0:T(8,128)(2,1)} %constant_dynamic-update-slice_fusion.5, bf16[512,1024]{1,0:T(8,128)(2,1)} %collective-permute-done.2, s32[]{:T(128)S(6)} %select_n.141), kind=kLoop, calls=%fused_computation.52 | loop fusion | bytes 2097156 | tf_op jit(solution)/shard_map/dynamic_update_slice | solution.py:20
  51.3 2.3 %constant_dynamic-update-slice_fusion.3 = bf16[512,8192]{1,0:T(8,128)(2,1)} fusion(bf16[512,8192]{1,0:T(8,128)(2,1)} %constant_dynamic-update-slice_fusion.4, bf16[512,1024]{1,0:T(8,128)(2,1)} %collective-permute-done.3, s32[]{:T(128)S(6)} %select_n.143), kind=kLoop, calls=%fused_computation.51 | loop fusion | bytes 2097156 | tf_op jit(solution)/shard_map/dynamic_update_slice | solution.py:25
  53.6 2.3 %constant_dynamic-update-slice_fusion.2 = bf16[512,8192]{1,0:T(8,128)(2,1)} fusion(bf16[512,8192]{1,0:T(8,128)(2,1)} %constant_dynamic-update-slice_fusion.3, bf16[512,1024]{1,0:T(8,128)(2,1)} %collective-permute-done.4, s32[]{:T(128)S(6)} %select_n.145), kind=kLoop, calls=%fused_computation.50 | loop fusion | bytes 2097156 | tf_op jit(solution)/shard_map/dynamic_update_slice | solution.py:20
  55.8 2.7 %collective-permute-done.5 = bf16[512,1024]{1,0:T(8,128)(2,1)S(1)} collective-permute-done((bf16[512,1024]{1,0:T(8,128)(2,1)}, bf16[512,1024]{1,0:T(8,128)(2,1)S(1)}, u32[]{:S(2)}, u32[]{:S(2)}) %collective-permute-start.5) | collective-permute-done | bytes 1048608 | tf_op jit(solution)/shard_map/ppermute | solution.py:24
  58.6 1.1 constant_dynamic-update-slice_fusion.1
  59.6 2.8 %collective-permute-done.6 = bf16[512,1024]{1,0:T(8,128)(2,1)S(1)} collective-permute-done((bf16[512,1024]{1,0:T(8,128)(2,1)}, bf16[512,1024]{1,0:T(8,128)(2,1)S(1)}, u32[]{:S(2)}, u32[]{:S(2)}) %collective-permute-start.6) | collective-permute-done | bytes 1048608 | tf_op jit(solution)/shard_map/ppermute | solution.py:19
  62.5 1.1 constant_dynamic-update-slice_fusion
  63.5 5.8 %fusion.7 = f32[512,256]{0,1:T(8,128)S(1)} fusion(bf16[8192,128]{1,0:T(8,128)(2,1)S(1)} %copy-done.3, bf16[8192,128]{1,0:T(8,128)(2,1)S(1)} %copy-done.4, bf16[512,8192]{1,0:T(8,128)(2,1)} %constant_dynamic-update-slice_fusion, f32[8192]{0:T(1024)S(1)} %copy-done.5, f32[512]{0:T(512)S(1)} %add_rsqrt_fusion), kind=kOutput, calls=%fused_computation.10 | convolution fusion | flops 2168586240 | bytes 13142016 | tf_op jit(solution)/shard_map/dot_general | solution.py:127
  71.2 9.8 %all-to-all-start.1 = ((f32[32,2,512]{2,1,0:T(2,128)}), f32[32,2,512]{2,1,0:T(2,128)S(1)}, u32[]{:S(2)}, u32[]{:S(2)}) async-start(f32[32,2,512]{2,1,0:T(2,128)} %broadcast_in_dim.48), calls=%async_computation.1 | async-start | bytes 262144 | tf_op jit(solution)/shard_map/all_to_all | solution.py:33
  82.5 8.9 %all-to-all-done.1 = f32[32,2,512]{2,1,0:T(2,128)S(1)} async-done(((f32[32,2,512]{2,1,0:T(2,128)}), f32[32,2,512]{2,1,0:T(2,128)S(1)}, u32[]{:S(2)}, u32[]{:S(2)}) %all-to-all-start.1) | async-done | bytes 131104 | tf_op jit(solution)/shard_map/all_to_all | solution.py:33
  93.1 1.3 %collective-permute-start.7 = (f32[7]{0:T(128)S(1)}, f32[7]{0:T(128)S(1)}, u32[]{:S(2)}, u32[]{:S(2)}) collective-permute-start(f32[7]{0:T(128)S(1)} %get-tuple-element.23), channel_id=1, source_target_pairs={{8,0},{16,8},{24,16},{32,24},{40,32},{48,40},{56,48},{64,56},{72,6... | collective-permute-start | bytes 92 | tf_op jit(solution)/shard_map/ppermute | solution.py:78
  94.4 4.5 %collective-permute-start.8 = (f32[7]{0:T(128)S(1)}, f32[7]{0:T(128)S(1)}, u32[]{:S(2)}, u32[]{:S(2)}) collective-permute-start(f32[7]{0:T(128)S(1)} %get-tuple-element.24), channel_id=1, source_target_pairs={{0,8},{8,16},{16,24},{24,32},{32,40},{40,48},{48,56},{56,64},{64,7... | collective-permute-start | bytes 92 | tf_op jit(solution)/shard_map/ppermute | solution.py:77
  98.9 1.3 %collective-permute-done.8 = f32[7]{0:T(128)S(1)} collective-permute-done((f32[7]{0:T(128)S(1)}, f32[7]{0:T(128)S(1)}, u32[]{:S(2)}, u32[]{:S(2)}) %collective-permute-start.8) | collective-permute-done | bytes 60 | tf_op jit(solution)/shard_map/ppermute | solution.py:77
  101.1 7.5 %all-to-all-start.2 = ((f32[32,1,4]{2,1,0:T(1,128)}), f32[32,1,4]{2,1,0:T(1,128)S(1)}, u32[]{:S(2)}, u32[]{:S(2)}) async-start(f32[32,1,4]{2,1,0:T(1,128)} %broadcast_in_dim.50), calls=%async_computation.2 | async-start | bytes 32768 | tf_op jit(solution)/shard_map/all_to_all | solution.py:33
  109.3 9.2 %all-to-all-done.2 = f32[32,1,4]{2,1,0:T(1,128)S(1)} async-done(((f32[32,1,4]{2,1,0:T(1,128)}), f32[32,1,4]{2,1,0:T(1,128)S(1)}, u32[]{:S(2)}, u32[]{:S(2)}) %all-to-all-start.2) | async-done | bytes 544 | tf_op jit(solution)/shard_map/all_to_all | solution.py:33
  118.6 2.6 %sort.15 = (f32[128]{0:T(128)S(1)}, s32[128]{0:T(128)}) sort(f32[128]{0:T(128)S(1)} %neg.20, s32[128]{0:T(128)S(1)} %iota.29), dimensions={0}, to_apply=%region_6.7 | sort | flops 896 | bytes 2048 | tf_op jit(solution)/shard_map/jit(sort)/sort | solution.py:163
  (77 shorter events, 8.9 us)
Async XLA Ops:
  0.6 44.1 %copy-start = (bf16[512,1024]{1,0:T(8,128)(2,1)S(1)}, bf16[512,1024]{1,0:T(8,128)(2,1)}, u32[]{:S(2)}) copy-start(bf16[512,1024]{1,0:T(8,128)(2,1)} %param.8) | copy-start | bytes 3145732
  0.6 45.4 %copy-start.1 = (bf16[64,1024]{1,0:T(8,128)(2,1)S(1)}, bf16[64,1024]{1,0:T(8,128)(2,1)}, u32[]{:S(2)}) copy-start(bf16[64,1024]{1,0:T(8,128)(2,1)} %param.12) | copy-start | bytes 393220
  0.6 14.4 %collective-permute-start = (bf16[512,1024]{1,0:T(8,128)(2,1)}, bf16[512,1024]{1,0:T(8,128)(2,1)S(1)}, u32[]{:S(2)}, u32[]{:S(2)}) collective-permute-start(bf16[512,1024]{1,0:T(8,128)(2,1)} %param.8), channel_id=1, source_target_pairs={{0,1},{1,2},{2,3},{3,4},{4,5},{5,6},{6,7},{7,0},{8,9},{9,10},{10,1... | collective-permute-start | bytes 3145736 | tf_op jit(solution)/shard_map/ppermute | solution.py:19
  0.7 14.4 %collective-permute-start.1 = (bf16[512,1024]{1,0:T(8,128)(2,1)}, bf16[512,1024]{1,0:T(8,128)(2,1)S(1)}, u32[]{:S(2)}, u32[]{:S(2)}) collective-permute-start(bf16[512,1024]{1,0:T(8,128)(2,1)} %param.8), channel_id=1, source_target_pairs={{0,7},{1,0},{2,1},{3,2},{4,3},{5,4},{6,5},{7,6},{8,15},{9,8},{10,9... | collective-permute-start | bytes 3145736 | tf_op jit(solution)/shard_map/ppermute | solution.py:24
  15.1 14.3 %collective-permute-start.2 = (bf16[512,1024]{1,0:T(8,128)(2,1)S(1)}, bf16[512,1024]{1,0:T(8,128)(2,1)}, u32[]{:S(2)}, u32[]{:S(2)}) collective-permute-start(bf16[512,1024]{1,0:T(8,128)(2,1)S(1)} %collective-permute-done), channel_id=1, source_target_pairs={{0,1},{1,2},{2,3},{3,4},{4,5},{5,6},{6,7},{7,0},{8,9},{9,10},{10,1... | collective-permute-start | bytes 3145736 | tf_op jit(solution)/shard_map/ppermute | solution.py:19
  15.1 30.6 %collective-permute-start.3 = (bf16[512,1024]{1,0:T(8,128)(2,1)S(1)}, bf16[512,1024]{1,0:T(8,128)(2,1)}, u32[]{:S(2)}, u32[]{:S(2)}) collective-permute-start(bf16[512,1024]{1,0:T(8,128)(2,1)S(1)} %collective-permute-done.1), channel_id=1, source_target_pairs={{0,7},{1,0},{2,1},{3,2},{4,3},{5,4},{6,5},{7,6},{8,15},{9,8},{10,9... | collective-permute-start | bytes 3145736 | tf_op jit(solution)/shard_map/ppermute | solution.py:24
  29.4 17.0 %collective-permute-start.4 = (bf16[512,1024]{1,0:T(8,128)(2,1)}, bf16[512,1024]{1,0:T(8,128)(2,1)}, u32[]{:S(2)}, u32[]{:S(2)}) collective-permute-start(bf16[512,1024]{1,0:T(8,128)(2,1)} %collective-permute-done.2), channel_id=1, source_target_pairs={{0,1},{1,2},{2,3},{3,4},{4,5},{5,6},{6,7},{7,0},{8,9},{9,10},{10,1... | collective-permute-start | bytes 3145736 | tf_op jit(solution)/shard_map/ppermute | solution.py:19
  31.5 14.8 %all-to-all-start = ((f32[8,1,512]{2,1,0:T(1,128)}), f32[8,1,512]{2,1,0:T(1,128)S(1)}, u32[]{:S(2)}, u32[]{:S(2)}) async-start(f32[8,1,512]{2,1,0:T(1,128)} %broadcast_in_dim.46), calls=%async_computation | async-start | bytes 32768 | tf_op jit(solution)/shard_map/all_to_all | solution.py:33
  44.7 18.8 %copy-start.5 = (f32[8192]{0:T(1024)S(1)}, f32[8192]{0:T(1024)}, u32[]{:S(2)}) copy-start(f32[8192]{0:T(1024)} %param.9) | copy-start | bytes 98308
  45.7 12.8 %collective-permute-start.5 = (bf16[512,1024]{1,0:T(8,128)(2,1)}, bf16[512,1024]{1,0:T(8,128)(2,1)S(1)}, u32[]{:S(2)}, u32[]{:S(2)}) collective-permute-start(bf16[512,1024]{1,0:T(8,128)(2,1)} %collective-permute-done.3), channel_id=1, source_target_pairs={{0,7},{1,0},{2,1},{3,2},{4,3},{5,4},{6,5},{7,6},{8,15},{9,8},{10,9... | collective-permute-start | bytes 3145736 | tf_op jit(solution)/shard_map/ppermute | solution.py:24
  46.4 17.1 %copy-start.3 = (bf16[8192,128]{1,0:T(8,128)(2,1)S(1)}, bf16[8192,128]{1,0:T(8,128)(2,1)}, u32[]{:S(2)}) copy-start(bf16[8192,128]{1,0:T(8,128)(2,1)} %param.11) | copy-start | bytes 6291460
  46.4 17.1 %copy-start.4 = (bf16[8192,128]{1,0:T(8,128)(2,1)S(1)}, bf16[8192,128]{1,0:T(8,128)(2,1)}, u32[]{:S(2)}) copy-start(bf16[8192,128]{1,0:T(8,128)(2,1)} %param.10) | copy-start | bytes 6291460
  46.4 16.0 %collective-permute-start.6 = (bf16[512,1024]{1,0:T(8,128)(2,1)}, bf16[512,1024]{1,0:T(8,128)(2,1)S(1)}, u32[]{:S(2)}, u32[]{:S(2)}) collective-permute-start(bf16[512,1024]{1,0:T(8,128)(2,1)} %collective-permute-done.4), channel_id=1, source_target_pairs={{0,1},{1,2},{2,3},{3,4},{4,5},{5,6},{6,7},{7,0},{8,9},{9,10},{10,1... | collective-permute-start | bytes 3145736 | tf_op jit(solution)/shard_map/ppermute | solution.py:19
  71.2 20.2 %all-to-all-start.1 = ((f32[32,2,512]{2,1,0:T(2,128)}), f32[32,2,512]{2,1,0:T(2,128)S(1)}, u32[]{:S(2)}, u32[]{:S(2)}) async-start(f32[32,2,512]{2,1,0:T(2,128)} %broadcast_in_dim.48), calls=%async_computation.1 | async-start | bytes 262144 | tf_op jit(solution)/shard_map/all_to_all | solution.py:33
  93.1 5.9 %collective-permute-start.7 = (f32[7]{0:T(128)S(1)}, f32[7]{0:T(128)S(1)}, u32[]{:S(2)}, u32[]{:S(2)}) collective-permute-start(f32[7]{0:T(128)S(1)} %get-tuple-element.23), channel_id=1, source_target_pairs={{8,0},{16,8},{24,16},{32,24},{40,32},{48,40},{56,48},{64,56},{72,6... | collective-permute-start | bytes 92 | tf_op jit(solution)/shard_map/ppermute | solution.py:78
  94.4 5.8 %collective-permute-start.8 = (f32[7]{0:T(128)S(1)}, f32[7]{0:T(128)S(1)}, u32[]{:S(2)}, u32[]{:S(2)}) collective-permute-start(f32[7]{0:T(128)S(1)} %get-tuple-element.24), channel_id=1, source_target_pairs={{0,8},{8,16},{16,24},{24,32},{32,40},{40,48},{48,56},{56,64},{64,7... | collective-permute-start | bytes 92 | tf_op jit(solution)/shard_map/ppermute | solution.py:77
  100.5 22.8 %copy-start.2 = (f32[4]{0:T(128)}, f32[4]{0:T(128)S(1)}, u32[]{:S(2)}) copy-start(f32[4]{0:T(128)S(1)} %bitcast_reduce_fusion) | copy-start | bytes 52
  101.1 17.3 %all-to-all-start.2 = ((f32[32,1,4]{2,1,0:T(1,128)}), f32[32,1,4]{2,1,0:T(1,128)S(1)}, u32[]{:S(2)}, u32[]{:S(2)}) async-start(f32[32,1,4]{2,1,0:T(1,128)} %broadcast_in_dim.50), calls=%async_computation.2 | async-start | bytes 32768 | tf_op jit(solution)/shard_map/all_to_all | solution.py:33
